TPU v7x, 32 devices: a whole 2x2x4 slice. The times are simulated.
32 devices in a mesh: section: 8 (over z, x), expert: 4 (over y, core).
Axes of the slice: x: 2, y: 2, z: 4, core: 2. Of those that a mesh axis runs over, the one named last changes fastest.
Arguments:
- entering: bfloat16 [2, 2, 128, 3584], P(None, None, 'expert'), may hold values from -6 to 6
- norm_gain: float32 [8, 3584], P('section'), may hold values from 0.5 to 1.5
- w_gate: bfloat16 [8, 3584, 2048], P('section', None, 'expert'), may hold values from -0.09375 to 0.09375
- w_up: bfloat16 [8, 3584, 2048], P('section', None, 'expert'), may hold values from -0.09375 to 0.09375
- w_down: bfloat16 [8, 2048, 3584], P('section', 'expert'), may hold values from -0.1875 to 0.1875
- route_ids: int32 [2, 2, 8, 128, 8], P(None, None, 'section', 'expert'), may hold values from 0 to 255, as said below
- route_scores: float32 [2, 2, 8, 128, 8], P(None, None, 'section', 'expert'), may hold values from 0.05 to 1
Outputs:
- leaving: bfloat16 [2, 2, 128, 3584], P(None, None, 'expert', 'section')
Inputs may be any that keep to these rules, and one draw needn't show every extreme that they name: `route_ids`: A token's 8 ids are distinct. In every block of 32 tokens (one direction, micro-batch and layer), at most 2 tokens name any one expert below 2, and in every such block exactly 2 tokens name one of them.
All inputs are finite; a program needn't handle non-finite values.
Results may differ from a plain program's by a relative error of at most 0.0072.
Values may be sent and summed in bfloat16 or wider, within the bound.
No kernel may reach another device: no remote copies, remote signals or barrier semaphores. Data moves between devices by JAX's collectives and lax.ppermute only.
A program may use at most 64 MiB of HBM per device.

v0:
```python
import functools

import jax
import jax.numpy as jnp
from jax import lax
from jax.experimental import pallas as pl
from jax.experimental.pallas import tpu as pltpu
from jax.sharding import PartitionSpec as P

GROUP = 2
CAP = 2

norm_eps = 1e-06
route_scale = 2.5

F32 = jnp.float32
BF16 = jnp.bfloat16
LANES = 128
AXES = ("section", "expert")

VMEM = pltpu.VMEM
HBM = pltpu.HBM
SMEM = pltpu.SMEM


def iota(shape, dim):
    return lax.broadcasted_iota(jnp.int32, shape, dim)


def start(*copies):
    for copy in copies:
        copy.start()
    return copies


def mm(a, b):
    return jnp.dot(a, b, preferred_element_type=F32)


def route_kernel(me_ref, ids_hbm, scores_hbm, x_hbm, *refs, window, slots):
    spread = len(refs) - 5
    outs = refs[:spread]
    ids_ref, scores_ref, x_ref, rows_ref, sems = refs[spread:]
    pairs = ((ids_hbm, ids_ref), (scores_hbm, scores_ref), (x_hbm, x_ref))
    copies = start(*[pltpu.make_async_copy(a, b, sems.at[n]) for n, (a, b) in enumerate(pairs)])
    groups, topk, tokens = ids_ref.shape
    count, width = x_ref.shape
    block_of = lambda v: jnp.floor((v.astype(F32) + 0.5) * (1.0 / tokens))
    place_i = iota((count, count), 0)
    place_j = iota((count, count), 1)
    earlier = ((place_i < place_j) & (block_of(place_i) == block_of(place_j))).astype(BF16)
    token_lane = iota((slots, count), 1).astype(F32)
    slot_row = iota((slots, count), 0).astype(F32)
    base = block_of(iota((1, count), 1)) * CAP
    meta_lane = iota((slots, LANES), 1)
    copies[0].wait()
    copies[1].wait()
    across = lambda ref: jnp.concatenate([ref[g] for g in range(groups)], axis=1)
    ids = across(ids_ref)
    scores = across(scores_ref)
    weights = route_scale * scores / jnp.sum(scores, axis=0, keepdims=True)
    same = [ids == e for e in range(window)]
    hits = jnp.concatenate([jnp.sum(jnp.where(m, 1.0, 0.0), axis=0, keepdims=True) for m in same], axis=0)
    before = mm(hits.astype(BF16), earlier)
    picks = []
    for e in range(window):
        share = jnp.sum(jnp.where(same[e], weights, 0.0), axis=0, keepdims=True)
        pick = jnp.where(base + before[e:e + 1] == slot_row, hits[e:e + 1], 0.0)
        picks.append(pick.astype(BF16))
        token = jnp.sum(pick * token_lane + pick, axis=-1, keepdims=True) - 1.0
        w = jnp.sum(pick * share, axis=-1, keepdims=True)
        high = w.astype(BF16).astype(F32)
        mid = (w - high).astype(BF16).astype(F32)
        low = w - high - mid
        meta = jnp.where(meta_lane == 0, token, 0.0)
        meta = jnp.where(meta_lane == 1, high, meta)
        meta = jnp.where(meta_lane == 2, mid, meta)
        meta = jnp.where(meta_lane == 3, low, meta)
        rows_ref[e, :, width:] = meta.astype(BF16)
    copies[2].wait()
    x = x_ref[...]
    for e in range(window):
        rows_ref[e, :, :width] = mm(picks[e], x).astype(BF16)
    me = me_ref[0]
    for k in range(spread):
        peer = lax.rem(me + k, spread)
        outs[k][...] = rows_ref[lax.div(peer, GROUP)]


def load_kernel(section_ref, x_hbm, wg_hbm, wu_hbm, own_ref, wg_ref, wu_ref, piece_ref, sems, *, feats):
    section = section_ref[0]
    tokens, padded = own_ref.shape
    span = piece_ref.shape[1]
    width = x_hbm.shape[1]
    first = jnp.minimum(lax.div(section * feats, LANES), (width - span) // LANES) * LANES
    piece, *weights = start(
        pltpu.make_async_copy(x_hbm.at[:, pl.ds(pl.multiple_of(first, LANES), span)], piece_ref, sems.at[0]),
        pltpu.make_async_copy(wg_hbm, wg_ref, sems.at[1]),
        pltpu.make_async_copy(wu_hbm, wu_ref, sems.at[2]),
    )
    piece.wait()
    moved = pltpu.roll(piece_ref[...].astype(F32), lax.rem(span - (section * feats - first), span), 1)[:, :padded]
    own_ref[...] = jnp.where(iota((tokens, padded), 1) < feats, moved, 0.0).astype(BF16)
    for weight in weights:
        weight.wait()


def silu_times(gate, up):
    return (gate / (1.0 + jnp.exp(-gate)) * up).astype(BF16)


def first_kernel(me_ref, gain_ref, wg_ref, wu_ref, wd_hbm, *refs, sections, feats):
    spread = len(refs) - 3
    ins, out_ref, wd_ref, sems = refs[:spread], refs[spread], refs[spread + 1], refs[spread + 2]
    copy, = start(pltpu.make_async_copy(wd_hbm, wd_ref, sems.at[0]))
    width = gain_ref.shape[1]
    slots = ins[0].shape[0]
    room = out_ref.shape[2] - feats
    x = jnp.concatenate([r[:, :width].astype(F32) for r in ins], axis=0)
    mean = jnp.mean(x * x, axis=-1, keepdims=True)
    h = (x * lax.rsqrt(mean + norm_eps) * gain_ref[...]).astype(BF16)
    act = silu_times(mm(h, wg_ref[...]), mm(h, wu_ref[...]))
    copy.wait()
    part = mm(act, wd_ref[...]).astype(BF16)
    me = me_ref[0]
    for k in range(spread):
        block = lax.rem(me - k + spread, spread)
        meta = ins[k][:, width:width + room]
        for s in range(sections):
            out_ref[s * spread + block, :, :feats] = part[k * slots:(k + 1) * slots, s * feats:(s + 1) * feats]
            out_ref[s * spread + block, :, feats:] = meta


def all_layers(pieces, gain_ref, wg_ref, wu_ref, wd_ref):
    rows, feats = pieces[0].shape
    total = jnp.zeros((rows, 1), F32)
    for piece in pieces:
        total = total + jnp.sum(piece * piece, axis=-1, keepdims=True)
    scale = lax.rsqrt(total * (1.0 / (feats * len(pieces))) + norm_eps)
    gate = jnp.zeros((rows, wg_ref.shape[1]), F32)
    up = jnp.zeros((rows, wg_ref.shape[1]), F32)
    for s, piece in enumerate(pieces):
        here = slice(s * feats, (s + 1) * feats)
        h = (piece * scale * gain_ref[:, here]).astype(BF16)
        gate = gate + mm(h, wg_ref[here, :])
        up = up + mm(h, wu_ref[here, :])
    return mm(silu_times(gate, up), wd_ref[...])


def write_flags(more_full, more, notes):
    top = jnp.max(notes, axis=0, keepdims=True)
    following = top[:, 1:2] + 1.0
    more_full[0] = jnp.max(jnp.where(following < top[:, 2:3], 1.0, 0.0)).astype(jnp.int32)
    more[0] = jnp.max(jnp.where(following < top[:, 0:1], 1.0, 0.0)).astype(jnp.int32)


def round_kernel(gain_ref, wg_ref, wu_ref, wd_ref, in_ref, out_ref, more_full, more, *, sections, feats):
    count, slots, padded = in_ref.shape
    spread = count // sections
    rows = spread * slots
    block = lambda s: in_ref[s * spread:(s + 1) * spread, :, :].astype(F32).reshape(rows, padded)
    write_flags(more_full, more, block(0)[:, feats:feats + 3])
    pieces = [block(s)[:, :feats] for s in range(sections)]
    part = all_layers(pieces, gain_ref, wg_ref, wu_ref, wd_ref).astype(BF16)
    for s in range(sections):
        piece = part[:, s * feats:(s + 1) * feats]
        for b in range(spread):
            out_ref[s * spread + b, :, :feats] = piece[b * slots:(b + 1) * slots]
            out_ref[s * spread + b, :, feats:] = jnp.zeros((slots, padded - feats), BF16)


def compact_round_kernel(gain_ref, wg_ref, wu_ref, wd_ref, in_ref, out_ref, more_full, more, wide_ref, *, sections, feats, tiles):
    count, sub, lanes = in_ref.shape
    spread = count // sections
    rows = spread * (sub // tiles)
    span = spread * sub
    wide_ref[...] = in_ref[...].astype(F32).reshape(count * sub, lanes)
    at = lambda s, k: pl.ds(s * span + k, rows, stride=tiles)
    spare = feats - (tiles - 1) * lanes
    write_flags(more_full, more, wide_ref[at(0, tiles - 1), :][:, spare:spare + 3])
    pieces = []
    for s in range(sections):
        pieces.append(jnp.concatenate([wide_ref[at(s, k), :] for k in range(tiles)], axis=1)[:, :feats])
    part = all_layers(pieces, gain_ref, wg_ref, wu_ref, wd_ref)
    for s in range(sections):
        piece = part[:, s * feats:(s + 1) * feats]
        piece = jnp.concatenate([piece, jnp.zeros((rows, tiles * lanes - feats), F32)], axis=1)
        for k in range(tiles):
            wide_ref[at(s, k), :] = piece[:, k * lanes:(k + 1) * lanes]
    out_ref[...] = wide_ref[...].reshape(count, sub, lanes).astype(BF16)


def add_parts(chosen, weights, parts, x, step, feats):
    tokens, padded = x.shape
    added = jnp.zeros((tokens, padded), F32)
    for w in weights:
        added = added + mm(jnp.where(chosen, w, 0.0).astype(BF16), parts)
    lane = iota((tokens, padded), 1)
    x = x.astype(F32)
    kept = jnp.where(lane == feats + 1, step + 1.0, x)
    return jnp.where(lane < feats, x + added, kept).astype(BF16)


def with_notes(rows, x, feats):
    return jnp.where(iota(rows.shape, 1) < feats, rows, x[0:1].astype(F32))


def gather_full(cols, x, send_ref, feats):
    count, slots, padded = send_ref.shape
    pick = (iota((count * slots, x.shape[0]), 1).astype(F32) == cols[:, 0:1]).astype(BF16)
    send_ref[...] = with_notes(mm(pick, x), x, feats).reshape(count, slots, padded).astype(BF16)


def gather_compact(cols, x, step, send_ref, table_ref, wide_ref, slots, feats, tiles):
    count, sub, lanes = send_ref.shape
    kept = sub // tiles
    lane = iota(cols.shape, 1)
    live = (cols[:, 4:5] == step) & (cols[:, 0:1] >= 0.0)
    values = jnp.where(lane == 0, cols + 1.0, cols)
    tables = []
    for c in range(kept):
        mine = jnp.where(live & (cols[:, 5:6] == c), values, 0.0)
        tables.append(jnp.sum(mine.reshape(count, slots, LANES), axis=1))
    table = jnp.concatenate(tables, axis=0)
    pick = (iota((kept * count, x.shape[0]), 1).astype(F32) + 1.0 == table[:, 0:1]).astype(BF16)
    rows = with_notes(mm(pick, x), x, feats)
    for c in range(kept):
        for k in range(tiles):
            wide_ref[pl.ds(c * tiles + k, count, stride=sub), :] = rows[c * count:(c + 1) * count, k * lanes:(k + 1) * lanes]
    send_ref[...] = wide_ref[...].reshape(count, sub, lanes).astype(BF16)
    table_ref[...] = table


def table_kernel(x_ref, in_ref, x_out, send_out, cols_out, rows_out, *, sections, feats, kept):
    count, slots, padded = in_ref.shape
    tokens = x_ref.shape[0]
    total = count * slots
    per = total // sections
    parts = in_ref[...].reshape(total, padded)
    meta = parts[:, feats:feats + 4].astype(F32)
    token = meta[:, 0:1]
    pick = (iota((total, tokens), 1).astype(F32) == token).astype(F32)
    hit = [jnp.minimum(jnp.sum(pick[l * per:(l + 1) * per], axis=0, keepdims=True), 1.0) for l in range(sections)]
    ahead, behind = [None] * sections, [None] * sections
    run_a = run_b = jnp.zeros((1, tokens), F32)
    for l in range(sections):
        ahead[l] = run_a
        run_a = run_a + hit[l]
        m = sections - 1 - l
        behind[m] = run_b
        run_b = run_b + hit[m]
    forward = iota((1, tokens), 1) < tokens // 2
    level = [
        jnp.sum(pick[l * per:(l + 1) * per] * jnp.where(forward, ahead[l], behind[l]), axis=-1, keepdims=True)
        for l in range(sections)
    ]
    level = jnp.concatenate(level, axis=0)
    depth = jnp.max(run_a, axis=-1, keepdims=True)
    lane = iota((total, LANES), 1)
    row = iota((total, LANES), 0)
    mine = jnp.where((lane.astype(F32) == level) & (token >= 0.0), 1.0, 0.0)
    seen = mine
    shift = 1
    slot = lax.rem(row, slots)
    while shift < slots:
        seen = seen + jnp.where(slot >= shift, pltpu.roll(seen, shift, 0), 0.0)
        shift *= 2
    seen = seen * mine
    rank = jnp.sum(seen, axis=-1, keepdims=True) - 1.0
    most = jnp.max(seen, axis=0, keepdims=True)
    level_lane = iota((1, LANES), 1).astype(F32)
    full = jnp.max(jnp.where(most > kept, level_lane + 1.0, 0.0), axis=-1, keepdims=True)
    cols = jnp.where(lane == 0, token, 0.0)
    for n in (1, 2, 3):
        cols = jnp.where(lane == n, meta[:, n:n + 1], cols)
    cols = jnp.where(lane == 4, level, cols)
    cols = jnp.where(lane == 5, rank, cols)
    rows_tab = cols.T[:8]
    cols_out[...] = cols
    rows_out[...] = rows_tab
    x_lane = iota((tokens, padded), 1)
    x = jnp.where(x_lane == feats, depth, x_ref[...].astype(F32))
    x = jnp.where(x_lane == feats + 2, full, x).astype(BF16)
    chosen = chosen_full(rows_tab, 0.0, tokens)
    x = add_parts(chosen, [rows_tab[n:n + 1] for n in (1, 2, 3)], parts, x, jnp.zeros((1, 1), F32), feats)
    x_out[...] = x
    gather_full(cols, x, send_out, feats)


def chosen_full(rows_tab, step, tokens):
    same = iota((tokens, rows_tab.shape[1]), 0).astype(F32) == rows_tab[0:1]
    return same & (rows_tab[4:5] == step)


def update_kernel(x_ref, in_ref, cols_ref, rows_ref, x_out, send_out, compact_out, table_out, wide_ref, *, feats, tiles):
    count, slots, padded = in_ref.shape
    x = x_ref[...]
    step = x[0:1, feats + 1:feats + 2].astype(F32)
    rows_tab = rows_ref[...]
    parts = in_ref[...].reshape(count * slots, padded)
    chosen = chosen_full(rows_tab, step, x.shape[0])
    x = add_parts(chosen, [rows_tab[n:n + 1] for n in (1, 2, 3)], parts, x, step, feats)
    x_out[...] = x
    cols = cols_ref[...]
    gather_full(cols, x, send_out, feats)
    gather_compact(cols, x, step + 1.0, compact_out, table_out, wide_ref, slots, feats, tiles)


def compact_update_kernel(x_ref, in_ref, cols_ref, tab_ref, x_out, send_out, table_out, wide_ref, *, slots, feats, tiles):
    count, sub, lanes = in_ref.shape
    kept = sub // tiles
    x = x_ref[...]
    step = x[0:1, feats + 1:feats + 2].astype(F32)
    wide_ref[...] = in_ref[...].astype(F32).reshape(count * sub, lanes)
    at = lambda c, k: pl.ds(c * tiles + k, count, stride=sub)
    parts = jnp.concatenate(
        [jnp.concatenate([wide_ref[at(c, k), :] for k in range(tiles)], axis=1) for c in range(kept)], axis=0
    ).astype(BF16)
    table = tab_ref[...].T[:8]
    chosen = iota((x.shape[0], table.shape[1]), 0).astype(F32) + 1.0 == table[0:1]
    x = add_parts(chosen, [table[n:n + 1] for n in (1, 2, 3)], parts, x, step, feats)
    x_out[...] = x
    gather_compact(cols_ref[...], x, step + 1.0, send_out, table_out, wide_ref, slots, feats, tiles)


def call(kernel, out_shape, in_spaces, out_spaces, name, scratch=(), limit=24 * 2**20, aliases={}):
    spec = lambda space: pl.BlockSpec(memory_space=space)
    single = not isinstance(out_shape, (list, tuple))
    return pl.pallas_call(
        kernel,
        out_shape=out_shape,
        in_specs=[spec(s) for s in in_spaces],
        out_specs=spec(out_spaces[0]) if single else [spec(s) for s in out_spaces],
        scratch_shapes=list(scratch),
        input_output_aliases=aliases,
        compiler_params=pltpu.CompilerParams(vmem_limit_bytes=limit),
        name=name,
    )


def on_device(entering, norm_gain, w_gate, w_up, w_down, route_ids, route_scores):
    sections = lax.axis_size("section")
    spread = lax.axis_size("expert")
    window = spread // GROUP
    ways, micro, tokens, width = entering.shape
    everyone = ways * micro * tokens
    slots = ways * micro * CAP
    feats = width // sections
    tiles = feats // LANES + 1
    padded = tiles * LANES
    devices = sections * spread
    kept = max(1, 8 // tiles)
    sub = kept * tiles
    by_token = lambda v: jnp.swapaxes(v[:, :, 0], 2, 3).reshape(ways * micro, v.shape[-1], tokens)
    scalar = lambda name: lax.axis_index(name).astype(jnp.int32).reshape(1)
    in_hbm = lambda v: pltpu.with_memory_space_constraint(v, HBM)
    in_vmem = lambda v: pltpu.with_memory_space_constraint(v, VMEM)
    sds = jax.ShapeDtypeStruct
    dma = pltpu.SemaphoreType.DMA

    me, section = scalar("expert"), scalar("section")
    flat = in_hbm(entering.reshape(everyone, width))
    ids, scores = in_hbm(by_token(route_ids)), in_hbm(by_token(route_scores))
    wg, wu, wd = [in_hbm(v[0]) for v in (w_gate, w_up, w_down)]
    resident = lambda v: VMEM(v.shape, v.dtype)

    rows = call(
        functools.partial(route_kernel, window=window, slots=slots),
        [sds((slots, width + LANES), BF16)] * spread,
        [SMEM] + [HBM] * 3,
        [VMEM] * spread,
        "route",
        scratch=[
            VMEM(ids.shape, ids.dtype),
            VMEM(scores.shape, scores.dtype),
            VMEM((everyone, width), BF16),
            VMEM((window, slots, width + LANES), BF16),
            dma((3,)),
        ],
    )(me, ids, scores, flat)
    received = [rows[0]] + [
        lax.ppermute(rows[k], "expert", [(y, (y + k) % spread) for y in range(spread)]) for k in range(1, spread)
    ]
    reach = max(s * feats % LANES for s in range(sections)) + feats
    span = -(-reach // LANES) * LANES
    state = sds((everyone, padded), BF16)
    own, wg, wu = call(
        functools.partial(load_kernel, feats=feats),
        [state, resident(wg), resident(wu)],
        [SMEM] + [HBM] * 3,
        [VMEM] * 3,
        "load",
        scratch=[VMEM((everyone, span), BF16), dma((3,))],
    )(section, flat, wg, wu)
    wg, wu = in_vmem(wg), in_vmem(wu)
    message = sds((devices, slots, padded), BF16)
    compact = sds((devices, sub, LANES), BF16)
    swap = lambda v: lax.all_to_all(v, AXES, split_axis=0, concat_axis=0, tiled=True)
    parts, wd = call(
        functools.partial(first_kernel, sections=sections, feats=feats),
        [message, resident(wd)],
        [SMEM] + [VMEM] * 3 + [HBM] + [VMEM] * spread,
        [VMEM] * 2,
        "first",
        scratch=[dma((1,))],
    )(me, norm_gain, wg, wu, wd, *received)
    experts = (norm_gain, wg, wu, in_vmem(wd))
    parts, own = lax.optimization_barrier((parts, own))
    x, send, cols, rows_tab = call(
        functools.partial(table_kernel, sections=sections, feats=feats, kept=kept),
        [state, message, sds((devices * slots, LANES), F32), sds((8, devices * slots), F32)],
        [VMEM, VMEM],
        [VMEM] * 4,
        "table",
    )(own, swap(parts))
    flag = SMEM((1,), jnp.int32)
    table_of = VMEM((devices * kept, LANES), F32)
    wide = VMEM((devices * sub, LANES), F32)

    def full_turn(x, send):
        parts, *flags = call(
            functools.partial(round_kernel, sections=sections, feats=feats),
            [message, flag, flag],
            [VMEM] * 5,
            [VMEM, SMEM, SMEM],
            "round",
        )(*experts, swap(send))
        x, send, packed, table = call(
            functools.partial(update_kernel, feats=feats, tiles=tiles),
            [state, message, compact, table_of],
            [VMEM] * 4,
            [VMEM] * 4,
            "update",
            aliases={0: 0},
            scratch=[wide],
        )(x, swap(parts), cols, rows_tab)
        return tuple(flags), x, send, packed, table

    def full_body(carry):
        carry = lax.optimization_barrier(carry)
        return full_turn(carry[1], carry[2])

    def compact_body(carry):
        unused, x, packed, table = lax.optimization_barrier(carry)
        parts, *flags = call(
            functools.partial(compact_round_kernel, sections=sections, feats=feats, tiles=tiles),
            [compact, flag, flag],
            [VMEM] * 5,
            [VMEM, SMEM, SMEM],
            "compact_round",
            scratch=[wide],
        )(*experts, swap(packed))
        x, packed, table = call(
            functools.partial(compact_update_kernel, slots=slots, feats=feats, tiles=tiles),
            [state, compact, table_of],
            [VMEM] * 4,
            [VMEM] * 3,
            "compact_update",
            aliases={0: 0, 3: 2},
            scratch=[wide],
        )(x, swap(parts), cols, in_vmem(table))
        return flags[1], x, packed, table

    carry = full_turn(x, send)
    carry = lax.while_loop(lambda c: c[0][0][0] > 0, full_body, carry)
    flags, x, send, packed, table = carry
    x = lax.while_loop(lambda c: c[0][0] > 0, compact_body, (flags[1], x, packed, table))[1]
    return x[:, :feats].reshape(ways, micro, tokens, feats)


def solution(mesh):
    return jax.shard_map(
        on_device,
        mesh=mesh,
        in_specs=(
            P(None, None, "expert", None),
            P("section", None),
            P("section", None, "expert"),
            P("section", None, "expert"),
            P("section", "expert", None),
            P(None, None, "section", "expert", None),
            P(None, None, "section", "expert", None),
        ),
        out_specs=P(None, None, "expert", "section"),
        check_vma=False,
    )
```

profile of v0, /device:TPU:0, one launch (start us, length us, event | category | flops | bytes accessed | tf_op | source)
XLA Modules:
  0.0 102.6 jit_solution(2490580662157959145)
XLA Ops:
  0.0 1.6 %route.1 = (bf16[8,3712]{1,0:T(8,128)(2,1)S(1)}, bf16[8,3712]{1,0:T(8,128)(2,1)S(1)}, bf16[8,3712]{1,0:T(8,128)(2,1)S(1)}, bf16[8,3712]{1,0:T(8,128)(2,1)S(1)}) custom-call(s32[1]{0:T(128)} %bitcast.6.me_ref, s32[4,8,32]{2,1,0:T(8,128)} %bitcast.26, f32[4,8,32]{2,1,0:T(8,128)} %bitcast.27, bf16[128,3584]{1,0:T(8,128)(2,1)} %bitcast.21), custom_call_target="tpu_custom_call" | custom-call | tf_op jit(solution)/shard_map/route/pallas_call | solution.py:367
  1.6 0.5 collective-permute-start
  2.2 2.6 %collective-permute-start.1 = (bf16[8,3712]{1,0:T(8,128)(2,1)S(1)}, bf16[8,3712]{1,0:T(8,128)(2,1)S(1)}, u32[]{:S(2)}, u32[]{:S(2)}) collective-permute-start(bf16[8,3712]{1,0:T(8,128)(2,1)S(1)} %get-tuple-element.155), channel_id=1, source_target_pairs={{0,2},{1,3},{2,0},{3,1},{4,6},{5,7},{6,4},{7,5},{8,10},{9,11},{10,... | collective-permute-start | bytes 178184 | tf_op jit(solution)/shard_map/ppermute | solution.py:382
  4.7 1.4 %collective-permute-start.2 = (bf16[8,3712]{1,0:T(8,128)(2,1)S(1)}, bf16[8,3712]{1,0:T(8,128)(2,1)S(1)}, u32[]{:S(2)}, u32[]{:S(2)}) collective-permute-start(bf16[8,3712]{1,0:T(8,128)(2,1)S(1)} %get-tuple-element.156), channel_id=1, source_target_pairs={{0,3},{1,0},{2,1},{3,2},{4,7},{5,4},{6,5},{7,6},{8,11},{9,8},{10,9... | collective-permute-start | bytes 178184 | tf_op jit(solution)/shard_map/ppermute | solution.py:382
  6.1 0.0 copy-start.1
  6.1 3.3 %load.1 = (bf16[128,512]{1,0:T(8,128)(2,1)S(1)}, bf16[3584,512]{1,0:T(8,128)(2,1)S(1)}, bf16[3584,512]{1,0:T(8,128)(2,1)S(1)}) custom-call(s32[1]{0:T(128)} %bitcast.2.section_ref, bf16[128,3584]{1,0:T(8,128)(2,1)} %bitcast.22, bf16[3584,512]{1,0:T(8,128)(2,1)} %bitcast.23, bf16[3584,512]{1,0:T(8,128)(2,1)} %bitcast.24), custom_call_target="tpu_custom_call" | custom-call | tf_op jit(solution)/shard_map/load/pallas_call | solution.py:387
  9.4 0.0 collective-permute-done.refs_1_
  9.4 0.0 collective-permute-done.1.refs_2_
  9.4 0.0 collective-permute-done.2.refs_3_
  9.4 0.0 copy-done.1
  9.4 2.9 %first.1 = (bf16[32,8,512]{2,1,0:T(8,128)(2,1)S(1)}, bf16[512,3584]{1,0:T(8,128)(2,1)S(1)}) custom-call(s32[1]{0:T(128)} %bitcast.6.me_ref, f32[1,3584]{1,0:T(1,128)S(1)} %copy-done.1, bf16[3584,512]{1,0:T(8,128)(2,1)S(1)} %get-tuple-element.282.wg_ref, bf16[3584,512]{1,0:T(8,128)(2,1)S(1)} %get-tuple-element.283.wu_ref, bf16[512,3584]{1,0:T(8,128)(2,1)} %bitcast.25, ...), custom_call_target="tpu_custom_call" | custom-call | tf_op jit(solution)/shard_map/first/pallas_call | solution.py:399
  12.3 15.3 %all_to_all.35.in_ref = bf16[32,8,512]{2,1,0:T(8,128)(2,1)S(1)} all-to-all(bf16[32,8,512]{2,1,0:T(8,128)(2,1)S(1)} %get-tuple-element.161), channel_id=1, replica_groups=mesh['section'=8,'expert'=4] {'section','expert'}, dimensions={0} | all-to-all | bytes 524288 | tf_op jit(solution)/shard_map/all_to_all | solution.py:398
  27.6 1.2 %table.1 = (bf16[128,512]{1,0:T(8,128)(2,1)S(1)}, bf16[32,8,512]{2,1,0:T(8,128)(2,1)S(1)}, f32[256,128]{1,0:T(8,128)S(1)}, f32[8,256]{1,0:T(8,128)S(1)}) custom-call(bf16[128,512]{1,0:T(8,128)(2,1)S(1)} %get-tuple-element.160.x_ref, bf16[32,8,512]{2,1,0:T(8,128)(2,1)S(1)} %all_to_all.35.in_ref), custom_call_target="tpu_custom_call" | custom-call | tf_op jit(solution)/shard_map/table/pallas_call | solution.py:409
  28.8 12.8 %all_to_all.36.in_ref = bf16[32,8,512]{2,1,0:T(8,128)(2,1)S(1)} all-to-all(bf16[32,8,512]{2,1,0:T(8,128)(2,1)S(1)} %get-tuple-element.162), channel_id=1, replica_groups=mesh['section'=8,'expert'=4] {'section','expert'}, dimensions={0} | all-to-all | bytes 524288 | tf_op jit(solution)/shard_map/all_to_all | solution.py:398
  41.6 2.3 %round.3 = (bf16[32,8,512]{2,1,0:T(8,128)(2,1)S(1)}, s32[1]{0:T(128)S(4)}, s32[1]{0:T(128)S(4)}) custom-call(f32[1,3584]{1,0:T(1,128)S(1)} %copy-done.1, bf16[3584,512]{1,0:T(8,128)(2,1)S(1)} %get-tuple-element.282.wg_ref, bf16[3584,512]{1,0:T(8,128)(2,1)S(1)} %get-tuple-element.283.wu_ref, bf16[512,3584]{1,0:T(8,128)(2,1)S(1)} %get-tuple-element.284.wd_ref, ...), custom_call_target="tpu_custom_call" | custom-call | tf_op jit(solution)/shard_map/round/pallas_call | solution.py:421
  43.9 12.8 %all_to_all.37.in_ref = bf16[32,8,512]{2,1,0:T(8,128)(2,1)S(1)} all-to-all(bf16[32,8,512]{2,1,0:T(8,128)(2,1)S(1)} %get-tuple-element.166), channel_id=1, replica_groups=mesh['section'=8,'expert'=4] {'section','expert'}, dimensions={0} | all-to-all | bytes 524288 | tf_op jit(solution)/shard_map/all_to_all | solution.py:398
  56.6 1.3 %update.3 = (bf16[128,512]{1,0:T(8,128)(2,1)S(1)}, bf16[32,8,512]{2,1,0:T(8,128)(2,1)S(1)}, bf16[32,8,128]{2,1,0:T(8,128)(2,1)}, f32[64,128]{1,0:T(8,128)S(1)}) custom-call(bf16[128,512]{1,0:T(8,128)(2,1)S(1)} %get-tuple-element.165.x_ref, bf16[32,8,512]{2,1,0:T(8,128)(2,1)S(1)} %all_to_all.37.in_ref, ...), custom_call_target="tpu_custom_call", output_to_operand_aliasing={{0}: (0, {})} | custom-call | tf_op jit(solution)/shard_map/update/pallas_call | solution.py:428
  57.9 44.1 %while.31 = (s32[1]{0:T(128)S(4)}, bf16[128,512]{1,0:T(8,128)(2,1)S(1)}, bf16[32,8,128]{2,1,0:T(8,128)(2,1)}, f32[64,128]{1,0:T(8,128)S(1)}, f32[1,3584]{1,0:T(1...) while((s32[1]{0:T(128)S(4)}, ...), condition=%region_3.0_spmd, body=%region_2.0_spmd | while | flops 1 | bytes 262225 | solution.py:467
  57.9 10.0 %all_to_all.33.in_ref = bf16[32,8,128]{2,1,0:T(8,128)(2,1)S(1)} all-to-all(bf16[32,8,128]{2,1,0:T(8,128)(2,1)} %get-tuple-element.114), channel_id=1, replica_groups=mesh['section'=8,'expert'=4] {'section','expert'}, dimensions={0} | all-to-all | bytes 131072 | tf_op jit(solution)/shard_map/while/body/all_to_all | solution.py:398
  67.9 1.8 %compact_round.1 = (bf16[32,8,128]{2,1,0:T(8,128)(2,1)S(1)}, s32[1]{0:T(128)S(4)}, s32[1]{0:T(128)S(4)}) custom-call(f32[1,3584]{1,0:T(1,128)S(1)} %get-tuple-element.299.gain_ref, bf16[3584,512]{1,0:T(8,128)(2,1)S(1)} %get-tuple-element.300.wg_ref, bf16[3584,512]{1,0:T(8,128)(2,1)S(1)} %get-tuple-element.301.wu_ref, ...), custom_call_target="tpu_custom_call" | custom-call | tf_op jit(solution)/shard_map/while/body/compact_round/pallas_call | solution.py:445
  69.7 9.1 %all_to_all.34.in_ref = bf16[32,8,128]{2,1,0:T(8,128)(2,1)S(1)} all-to-all(bf16[32,8,128]{2,1,0:T(8,128)(2,1)S(1)} %get-tuple-element.117), channel_id=1, replica_groups=mesh['section'=8,'expert'=4] {'section','expert'}, dimensions={0} | all-to-all | bytes 131072 | tf_op jit(solution)/shard_map/while/body/all_to_all | solution.py:398
  78.8 1.2 %compact_update.1 = (bf16[128,512]{1,0:T(8,128)(2,1)S(1)}, bf16[32,8,128]{2,1,0:T(8,128)(2,1)}, f32[64,128]{1,0:T(8,128)S(1)}) custom-call(bf16[128,512]{1,0:T(8,128)(2,1)S(1)} %get-tuple-element.116.x_ref, bf16[32,8,128]{2,1,0:T(8,128)(2,1)S(1)} %all_to_all.34.in_ref, ...), custom_call_target="tpu_custom_call", output_to_operand_aliasing={{0}: (0, {}), {2}: (3, {})} | custom-call | tf_op jit(solution)/shard_map/while/body/compact_update/pallas_call | solution.py:453
  79.9 10.0 %all_to_all.33.in_ref = bf16[32,8,128]{2,1,0:T(8,128)(2,1)S(1)} all-to-all(bf16[32,8,128]{2,1,0:T(8,128)(2,1)} %get-tuple-element.114), channel_id=1, replica_groups=mesh['section'=8,'expert'=4] {'section','expert'}, dimensions={0} | all-to-all | bytes 131072 | tf_op jit(solution)/shard_map/while/body/all_to_all | solution.py:398
  89.9 1.8 %compact_round.1 = (bf16[32,8,128]{2,1,0:T(8,128)(2,1)S(1)}, s32[1]{0:T(128)S(4)}, s32[1]{0:T(128)S(4)}) custom-call(f32[1,3584]{1,0:T(1,128)S(1)} %get-tuple-element.299.gain_ref, bf16[3584,512]{1,0:T(8,128)(2,1)S(1)} %get-tuple-element.300.wg_ref, bf16[3584,512]{1,0:T(8,128)(2,1)S(1)} %get-tuple-element.301.wu_ref, ...), custom_call_target="tpu_custom_call" | custom-call | tf_op jit(solution)/shard_map/while/body/compact_round/pallas_call | solution.py:445
  91.7 9.1 %all_to_all.34.in_ref = bf16[32,8,128]{2,1,0:T(8,128)(2,1)S(1)} all-to-all(bf16[32,8,128]{2,1,0:T(8,128)(2,1)S(1)} %get-tuple-element.117), channel_id=1, replica_groups=mesh['section'=8,'expert'=4] {'section','expert'}, dimensions={0} | all-to-all | bytes 131072 | tf_op jit(solution)/shard_map/while/body/all_to_all | solution.py:398
  100.8 1.2 %compact_update.1 = (bf16[128,512]{1,0:T(8,128)(2,1)S(1)}, bf16[32,8,128]{2,1,0:T(8,128)(2,1)}, f32[64,128]{1,0:T(8,128)S(1)}) custom-call(bf16[128,512]{1,0:T(8,128)(2,1)S(1)} %get-tuple-element.116.x_ref, bf16[32,8,128]{2,1,0:T(8,128)(2,1)S(1)} %all_to_all.34.in_ref, ...), custom_call_target="tpu_custom_call", output_to_operand_aliasing={{0}: (0, {}), {2}: (3, {})} | custom-call | tf_op jit(solution)/shard_map/while/body/compact_update/pallas_call | solution.py:453
  102.0 0.0 copy-start
  102.0 0.7 copy-done
  (1 shorter events, 0.0 us)
Async XLA Ops:
  1.6 7.8 %collective-permute-start = (bf16[8,3712]{1,0:T(8,128)(2,1)S(1)}, bf16[8,3712]{1,0:T(8,128)(2,1)S(1)}, u32[]{:S(2)}, u32[]{:S(2)}) collective-permute-start(bf16[8,3712]{1,0:T(8,128)(2,1)S(1)} %get-tuple-element.154), channel_id=1, source_target_pairs={{0,1},{1,2},{2,3},{3,0},{4,5},{5,6},{6,7},{7,4},{8,9},{9,10},{10,1... | collective-permute-start | bytes 178184 | tf_op jit(solution)/shard_map/ppermute | solution.py:382
  2.2 7.2 %collective-permute-start.1 = (bf16[8,3712]{1,0:T(8,128)(2,1)S(1)}, bf16[8,3712]{1,0:T(8,128)(2,1)S(1)}, u32[]{:S(2)}, u32[]{:S(2)}) collective-permute-start(bf16[8,3712]{1,0:T(8,128)(2,1)S(1)} %get-tuple-element.155), channel_id=1, source_target_pairs={{0,2},{1,3},{2,0},{3,1},{4,6},{5,7},{6,4},{7,5},{8,10},{9,11},{10,... | collective-permute-start | bytes 178184 | tf_op jit(solution)/shard_map/ppermute | solution.py:382
  4.7 4.7 %collective-permute-start.2 = (bf16[8,3712]{1,0:T(8,128)(2,1)S(1)}, bf16[8,3712]{1,0:T(8,128)(2,1)S(1)}, u32[]{:S(2)}, u32[]{:S(2)}) collective-permute-start(bf16[8,3712]{1,0:T(8,128)(2,1)S(1)} %get-tuple-element.156), channel_id=1, source_target_pairs={{0,3},{1,0},{2,1},{3,2},{4,7},{5,4},{6,5},{7,6},{8,11},{9,8},{10,9... | collective-permute-start | bytes 178184 | tf_op jit(solution)/shard_map/ppermute | solution.py:382
  6.1 3.3 %copy-start.1 = (f32[1,3584]{1,0:T(1,128)S(1)}, f32[1,3584]{1,0:T(1,128)}, u32[]{:S(2)}) copy-start(f32[1,3584]{1,0:T(1,128)} %gain_ref.3) | copy-start | bytes 43012
  102.0 0.7 copy-start
where the time goes:
time: 103 us
  blocking collectives  78.9 us (77%)
  Pallas kernels  18.4 us (18%)
  starting transfers between devices  4.52 us (4%)
    all_to_all x7, blocking collectives, on_device(): lax.all_to_all(v, AXES, split_axis=0, concat_axis=0, tiled=True)  78.9 us
    ppermute x3, starting transfers between devices, on_device(): lax.ppermute(rows[k], 'expert', [(y, (y + k) % spread) for y in range(spr...  4.52 us
    pallas_call x2, Pallas kernels, compact_body(): call(functools.partial(compact_round_kernel, sections=sections, feats=fea...  3.56 us
    pallas_call x1, Pallas kernels, on_device(): call(functools.partial(load_kernel, feats=feats), [state, resident(wg), r...  3.25 us
    pallas_call x1, Pallas kernels, on_device(): call(functools.partial(first_kernel, sections=sections, feats=feats), [me...  2.87 us
    pallas_call x2, Pallas kernels, compact_body(): call(functools.partial(compact_update_kernel, slots=slots, feats=feats, t...  2.37 us
    pallas_call x1, Pallas kernels, full_turn(): call(functools.partial(round_kernel, sections=sections, feats=feats), [me...  2.3 us
  transfers between devices with their start and end apart: 3, of which 0 were waited for; matrix products, arithmetic and copies ran while one was open for 0% of the time, Pallas kernels for 3%

commit v1 on v0

v1 whole, which is shorter than its diff:
```python
import functools

import jax
import jax.numpy as jnp
from jax import lax
from jax.experimental import pallas as pl
from jax.experimental.pallas import tpu as pltpu
from jax.sharding import PartitionSpec as P

GROUP = 2
CAP = 2

norm_eps = 1e-06
route_scale = 2.5

F32 = jnp.float32
BF16 = jnp.bfloat16
LANES = 128
AXES = ("section", "expert")

VMEM = pltpu.VMEM
HBM = pltpu.HBM
SMEM = pltpu.SMEM


def iota(shape, dim):
    return lax.broadcasted_iota(jnp.int32, shape, dim)


def start(*copies):
    for copy in copies:
        copy.start()
    return copies


def mm(a, b):
    return jnp.dot(a, b, preferred_element_type=F32)


def route_kernel(me_ref, ids_hbm, scores_hbm, x_hbm, *refs, window, slots):
    spread = len(refs) - 5
    outs = refs[:spread]
    ids_ref, scores_ref, x_ref, rows_ref, sems = refs[spread:]
    pairs = ((ids_hbm, ids_ref), (scores_hbm, scores_ref), (x_hbm, x_ref))
    copies = start(*[pltpu.make_async_copy(a, b, sems.at[n]) for n, (a, b) in enumerate(pairs)])
    groups, topk, tokens = ids_ref.shape
    count, width = x_ref.shape
    block_of = lambda v: jnp.floor((v.astype(F32) + 0.5) * (1.0 / tokens))
    place_i = iota((count, count), 0)
    place_j = iota((count, count), 1)
    earlier = ((place_i < place_j) & (block_of(place_i) == block_of(place_j))).astype(BF16)
    token_lane = iota((slots, count), 1).astype(F32)
    slot_row = iota((slots, count), 0).astype(F32)
    base = block_of(iota((1, count), 1)) * CAP
    meta_lane = iota((slots, LANES), 1)
    copies[0].wait()
    copies[1].wait()
    across = lambda ref: jnp.concatenate([ref[g] for g in range(groups)], axis=1)
    ids = across(ids_ref)
    scores = across(scores_ref)
    weights = route_scale * scores / jnp.sum(scores, axis=0, keepdims=True)
    same = [ids == e for e in range(window)]
    hits = jnp.concatenate([jnp.sum(jnp.where(m, 1.0, 0.0), axis=0, keepdims=True) for m in same], axis=0)
    before = mm(hits.astype(BF16), earlier)
    picks = []
    for e in range(window):
        share = jnp.sum(jnp.where(same[e], weights, 0.0), axis=0, keepdims=True)
        pick = jnp.where(base + before[e:e + 1] == slot_row, hits[e:e + 1], 0.0)
        picks.append(pick.astype(BF16))
        token = jnp.sum(pick * token_lane + pick, axis=-1, keepdims=True) - 1.0
        w = jnp.sum(pick * share, axis=-1, keepdims=True)
        high = w.astype(BF16).astype(F32)
        mid = (w - high).astype(BF16).astype(F32)
        low = w - high - mid
        meta = jnp.where(meta_lane == 0, token, 0.0)
        meta = jnp.where(meta_lane == 1, high, meta)
        meta = jnp.where(meta_lane == 2, mid, meta)
        meta = jnp.where(meta_lane == 3, low, meta)
        rows_ref[e, :, width:] = meta.astype(BF16)
    copies[2].wait()
    x = x_ref[...]
    for e in range(window):
        rows_ref[e, :, :width] = mm(picks[e], x).astype(BF16)
    me = me_ref[0]
    for k in range(spread):
        peer = lax.rem(me + k, spread)
        outs[k][...] = rows_ref[lax.div(peer, GROUP)]


def load_kernel(section_ref, x_hbm, wg_hbm, wu_hbm, own_ref, wg_ref, wu_ref, piece_ref, sems, *, feats):
    section = section_ref[0]
    tokens, padded = own_ref.shape
    span = piece_ref.shape[1]
    width = x_hbm.shape[1]
    first = jnp.minimum(lax.div(section * feats, LANES), (width - span) // LANES) * LANES
    piece, *weights = start(
        pltpu.make_async_copy(x_hbm.at[:, pl.ds(pl.multiple_of(first, LANES), span)], piece_ref, sems.at[0]),
        pltpu.make_async_copy(wg_hbm, wg_ref, sems.at[1]),
        pltpu.make_async_copy(wu_hbm, wu_ref, sems.at[2]),
    )
    piece.wait()
    moved = pltpu.roll(piece_ref[...].astype(F32), lax.rem(span - (section * feats - first), span), 1)[:, :padded]
    own_ref[...] = jnp.where(iota((tokens, padded), 1) < feats, moved, 0.0).astype(BF16)
    for weight in weights:
        weight.wait()


def silu_times(gate, up):
    return (gate / (1.0 + jnp.exp(-gate)) * up).astype(BF16)


def first_kernel(me_ref, gain_ref, wg_ref, wu_ref, wd_hbm, *refs, sections, feats):
    spread = len(refs) - 3
    ins, out_ref, wd_ref, sems = refs[:spread], refs[spread], refs[spread + 1], refs[spread + 2]
    copy, = start(pltpu.make_async_copy(wd_hbm, wd_ref, sems.at[0]))
    width = gain_ref.shape[1]
    slots = ins[0].shape[0]
    room = out_ref.shape[2] - feats
    x = jnp.concatenate([r[:, :width].astype(F32) for r in ins], axis=0)
    mean = jnp.mean(x * x, axis=-1, keepdims=True)
    h = (x * lax.rsqrt(mean + norm_eps) * gain_ref[...]).astype(BF16)
    act = silu_times(mm(h, wg_ref[...]), mm(h, wu_ref[...]))
    copy.wait()
    part = mm(act, wd_ref[...]).astype(BF16)
    me = me_ref[0]
    for k in range(spread):
        block = lax.rem(me - k + spread, spread)
        meta = ins[k][:, width:width + room]
        for s in range(sections):
            out_ref[s * spread + block, :, :feats] = part[k * slots:(k + 1) * slots, s * feats:(s + 1) * feats]
            out_ref[s * spread + block, :, feats:] = meta


def all_layers(pieces, gain_ref, wg_ref, wu_ref, wd_ref):
    rows, feats = pieces[0].shape
    total = jnp.zeros((rows, 1), F32)
    for piece in pieces:
        total = total + jnp.sum(piece * piece, axis=-1, keepdims=True)
    scale = lax.rsqrt(total * (1.0 / (feats * len(pieces))) + norm_eps)
    gate = jnp.zeros((rows, wg_ref.shape[1]), F32)
    up = jnp.zeros((rows, wg_ref.shape[1]), F32)
    for s, piece in enumerate(pieces):
        here = slice(s * feats, (s + 1) * feats)
        h = (piece * scale * gain_ref[:, here]).astype(BF16)
        gate = gate + mm(h, wg_ref[here, :])
        up = up + mm(h, wu_ref[here, :])
    return mm(silu_times(gate, up), wd_ref[...])


def round_kernel(gain_ref, wg_ref, wu_ref, wd_ref, in_ref, out_ref, more, wide_ref, *, sections, feats, tiles):
    count, sub, lanes = in_ref.shape
    spread = count // sections
    rows = spread * (sub // tiles)
    span = spread * sub
    wide_ref[...] = in_ref[...].astype(F32).reshape(count * sub, lanes)
    at = lambda s, k: pl.ds(s * span + k, rows, stride=tiles)
    spare = feats - (tiles - 1) * lanes
    more[0] = jnp.max(wide_ref[at(0, tiles - 1), :][:, spare:spare + 1]).astype(jnp.int32)
    pieces = []
    for s in range(sections):
        pieces.append(jnp.concatenate([wide_ref[at(s, k), :] for k in range(tiles)], axis=1)[:, :feats])
    part = all_layers(pieces, gain_ref, wg_ref, wu_ref, wd_ref)
    for s in range(sections):
        piece = part[:, s * feats:(s + 1) * feats]
        piece = jnp.concatenate([piece, jnp.zeros((rows, tiles * lanes - feats), F32)], axis=1)
        for k in range(tiles):
            wide_ref[at(s, k), :] = piece[:, k * lanes:(k + 1) * lanes]
    out_ref[...] = wide_ref[...].reshape(count, sub, lanes).astype(BF16)


def add_parts(table, parts, x, feats):
    tokens, padded = x.shape
    across = table.T[:8]
    chosen = iota((tokens, across.shape[1]), 0).astype(F32) + 1.0 == across[0:1]
    added = jnp.zeros((tokens, padded), F32)
    for n in (1, 2, 3):
        added = added + mm(jnp.where(chosen, across[n:n + 1], 0.0).astype(BF16), parts)
    return jnp.where(iota((tokens, padded), 1) < feats, x.astype(F32) + added, 0.0).astype(BF16)


def find_ready(cols, tokens, sections):
    per = cols.shape[0] // sections
    pick = (iota((cols.shape[0], tokens), 1).astype(F32) == cols[:, 0:1]).astype(F32)
    pending = cols[:, 4:5]
    layer = lambda v, l: v[l * per:(l + 1) * per]
    waits = [jnp.minimum(jnp.sum(layer(pick, l) * layer(pending, l), axis=0, keepdims=True), 1.0) for l in range(sections)]
    ahead, behind = [None] * sections, [None] * sections
    run_a = run_b = jnp.zeros((1, tokens), F32)
    for l in range(sections):
        ahead[l] = run_a
        run_a = run_a + waits[l]
        m = sections - 1 - l
        behind[m] = run_b
        run_b = run_b + waits[m]
    forward = iota((1, tokens), 1) < tokens // 2
    ready = []
    for l in range(sections):
        free = jnp.where(jnp.where(forward, ahead[l], behind[l]) == 0.0, waits[l], 0.0)
        ready.append(jnp.sum(layer(pick, l) * free, axis=-1, keepdims=True))
    return jnp.concatenate(ready, axis=0), pick


def values_of(cols, taken):
    lane = iota(cols.shape, 1)
    return jnp.where(taken & (lane < 4), jnp.where(lane == 0, cols + 1.0, cols), 0.0)


def take_next(cols, x, cols_ref, send_ref, table_ref, wide_ref, sections, slots, feats, tiles):
    count, sub, lanes = send_ref.shape
    kept = sub // tiles
    tokens, padded = x.shape
    total = cols.shape[0]
    per = total // sections
    ready, pick = find_ready(cols, tokens, sections)
    slot = lax.rem(iota((total, LANES), 0), slots)
    seen = jnp.broadcast_to(ready, (total, LANES))
    shift = 1
    while shift < slots:
        seen = seen + jnp.where(slot >= shift, pltpu.roll(seen, shift, 0), 0.0)
        shift *= 2
    late = jnp.where(seen[:, 0:1] > kept, ready, 0.0)
    held = []
    for l in range(sections):
        here = slice(l * per, (l + 1) * per)
        wait = jnp.sum(pick[here] * late[here], axis=0, keepdims=True)
        held.append(jnp.sum(pick[here] * wait, axis=-1, keepdims=True))
    taken = jnp.where(jnp.concatenate(held, axis=0) == 0.0, ready, 0.0)
    cols = jnp.where(iota((total, LANES), 1) == 4, cols - taken, cols)
    cols_ref[...] = cols
    left = jnp.max(cols[:, 4:5], axis=0, keepdims=True)
    group_of = lambda v, size: jnp.floor((v.astype(F32) + 0.5) * (1.0 / size))
    owner = (group_of(iota((count, total), 0), GROUP) == group_of(iota((count, total), 1), slots)).astype(BF16)
    tables = []
    for c in range(kept):
        mine = values_of(cols, (taken > 0.0) & (seen == c + 1.0))
        tables.append(mm(owner, mine.astype(BF16)))
    table = jnp.concatenate(tables, axis=0)
    table_ref[...] = table
    chosen = (iota((kept * count, tokens), 1).astype(F32) + 1.0 == table[:, 0:1]).astype(BF16)
    rows = jnp.where(iota((kept * count, padded), 1) == feats, left, mm(chosen, x))
    for c in range(kept):
        for k in range(tiles):
            wide_ref[pl.ds(c * tiles + k, count, stride=sub), :] = rows[c * count:(c + 1) * count, k * lanes:(k + 1) * lanes]
    send_ref[...] = wide_ref[...].reshape(count, sub, lanes).astype(BF16)


def table_kernel(x_ref, in_ref, x_out, cols_out, send_out, table_out, wide_ref, *, sections, feats, tiles):
    count, slots, padded = in_ref.shape
    tokens = x_ref.shape[0]
    groups = count // GROUP
    parts = in_ref[...].reshape(count * slots, padded)
    meta = [parts[g * GROUP * slots:(g * GROUP + 1) * slots, feats:feats + 4].astype(F32) for g in range(groups)]
    meta = jnp.concatenate(meta, axis=0)
    lane = iota((groups * slots, LANES), 1)
    cols = jnp.where(lane == 0, meta[:, 0:1], 0.0)
    for n in (1, 2, 3):
        cols = jnp.where(lane == n, meta[:, n:n + 1], cols)
    cols = jnp.where((lane == 4) & (meta[:, 0:1] >= 0.0), 1.0, cols)
    ready, unused = find_ready(cols, tokens, sections)
    mine = values_of(cols, ready > 0.0)
    table = jnp.concatenate([mine[g * slots:(g + 1) * slots] for g in range(groups) for n in range(GROUP)], axis=0)
    x = add_parts(table, parts, x_ref[...], feats)
    x_out[...] = x
    cols = jnp.where(lane == 4, cols - ready, cols)
    take_next(cols, x, cols_out, send_out, table_out, wide_ref, sections, slots, feats, tiles)


def update_kernel(x_ref, cols_ref, in_ref, tab_ref, x_out, cols_out, send_out, table_out, in_wide, out_wide, *, sections, slots, feats, tiles):
    count, sub, lanes = in_ref.shape
    in_wide[...] = in_ref[...].astype(F32).reshape(count * sub, lanes)
    at = lambda c, k: pl.ds(c * tiles + k, count, stride=sub)
    parts = jnp.concatenate(
        [jnp.concatenate([in_wide[at(c, k), :] for k in range(tiles)], axis=1) for c in range(sub // tiles)], axis=0
    ).astype(BF16)
    x = add_parts(tab_ref[...], parts, x_ref[...], feats)
    x_out[...] = x
    take_next(cols_ref[...], x, cols_out, send_out, table_out, out_wide, sections, slots, feats, tiles)


def call(kernel, out_shape, in_spaces, out_spaces, name, scratch=(), limit=24 * 2**20, aliases={}):
    spec = lambda space: pl.BlockSpec(memory_space=space)
    single = not isinstance(out_shape, (list, tuple))
    return pl.pallas_call(
        kernel,
        out_shape=out_shape,
        in_specs=[spec(s) for s in in_spaces],
        out_specs=spec(out_spaces[0]) if single else [spec(s) for s in out_spaces],
        scratch_shapes=list(scratch),
        input_output_aliases=aliases,
        compiler_params=pltpu.CompilerParams(vmem_limit_bytes=limit),
        name=name,
    )


def on_device(entering, norm_gain, w_gate, w_up, w_down, route_ids, route_scores):
    sections = lax.axis_size("section")
    spread = lax.axis_size("expert")
    window = spread // GROUP
    ways, micro, tokens, width = entering.shape
    everyone = ways * micro * tokens
    slots = ways * micro * CAP
    feats = width // sections
    tiles = feats // LANES + 1
    padded = tiles * LANES
    devices = sections * spread
    later_kept = max(1, 8 // tiles)
    early_kept = min(slots, 2 * later_kept)
    by_token = lambda v: jnp.swapaxes(v[:, :, 0], 2, 3).reshape(ways * micro, v.shape[-1], tokens)
    scalar = lambda name: lax.axis_index(name).astype(jnp.int32).reshape(1)
    in_hbm = lambda v: pltpu.with_memory_space_constraint(v, HBM)
    in_vmem = lambda v: pltpu.with_memory_space_constraint(v, VMEM)
    sds = jax.ShapeDtypeStruct
    dma = pltpu.SemaphoreType.DMA

    me, section = scalar("expert"), scalar("section")
    flat = in_hbm(entering.reshape(everyone, width))
    ids, scores = in_hbm(by_token(route_ids)), in_hbm(by_token(route_scores))
    wg, wu, wd = [in_hbm(v[0]) for v in (w_gate, w_up, w_down)]
    resident = lambda v: VMEM(v.shape, v.dtype)

    rows = call(
        functools.partial(route_kernel, window=window, slots=slots),
        [sds((slots, width + LANES), BF16)] * spread,
        [SMEM] + [HBM] * 3,
        [VMEM] * spread,
        "route",
        scratch=[
            VMEM(ids.shape, ids.dtype),
            VMEM(scores.shape, scores.dtype),
            VMEM((everyone, width), BF16),
            VMEM((window, slots, width + LANES), BF16),
            dma((3,)),
        ],
    )(me, ids, scores, flat)
    received = [rows[0]] + [
        lax.ppermute(rows[k], "expert", [(y, (y + k) % spread) for y in range(spread)]) for k in range(1, spread)
    ]
    reach = max(s * feats % LANES for s in range(sections)) + feats
    span = -(-reach // LANES) * LANES
    state = sds((everyone, padded), BF16)
    own, wg, wu = call(
        functools.partial(load_kernel, feats=feats),
        [state, resident(wg), resident(wu)],
        [SMEM] + [HBM] * 3,
        [VMEM] * 3,
        "load",
        scratch=[VMEM((everyone, span), BF16), dma((3,))],
    )(section, flat, wg, wu)
    wg, wu = in_vmem(wg), in_vmem(wu)
    message = sds((devices, slots, padded), BF16)
    compact = lambda kept: sds((devices, kept * tiles, LANES), BF16)
    swap = lambda v: lax.all_to_all(v, AXES, split_axis=0, concat_axis=0, tiled=True)
    parts, wd = call(
        functools.partial(first_kernel, sections=sections, feats=feats),
        [message, resident(wd)],
        [SMEM] + [VMEM] * 3 + [HBM] + [VMEM] * spread,
        [VMEM] * 2,
        "first",
        scratch=[dma((1,))],
    )(me, norm_gain, wg, wu, wd, *received)
    experts = (norm_gain, wg, wu, in_vmem(wd))
    parts, own = lax.optimization_barrier((parts, own))
    flag = SMEM((1,), jnp.int32)
    table_of = lambda kept: VMEM((devices * kept, LANES), F32)
    wide = lambda kept: VMEM((devices * kept * tiles, LANES), F32)
    cols_of = VMEM((devices // GROUP * slots, LANES), F32)
    sizes = dict(sections=sections, feats=feats, tiles=tiles)
    carry = call(
        functools.partial(table_kernel, **sizes),
        [state, cols_of, compact(early_kept), table_of(early_kept)],
        [VMEM] * 2,
        [VMEM] * 4,
        "table",
        scratch=[wide(early_kept)],
    )(own, swap(parts))

    def turn(x, cols, packed, table, kept):
        parts, more = call(
            functools.partial(round_kernel, **sizes),
            [compact(kept), flag],
            [VMEM] * 5,
            [VMEM, SMEM],
            "round",
            scratch=[wide(kept)],
        )(*experts, swap(packed))
        return more, *call(
            functools.partial(update_kernel, slots=slots, **sizes),
            [state, cols_of, compact(later_kept), table_of(later_kept)],
            [VMEM] * 4,
            [VMEM] * 4,
            "update",
            aliases={0: 0, 1: 1, 3: 3} if kept == later_kept else {0: 0, 1: 1},
            scratch=[wide(kept), wide(later_kept)],
        )(x, in_vmem(cols), swap(parts), in_vmem(table))

    def body(carry):
        return turn(*lax.optimization_barrier(carry)[1:], later_kept)

    carry = lax.while_loop(lambda c: c[0][0] > 0, body, turn(*carry, early_kept))
    x = carry[1]
    return x[:, :feats].reshape(ways, micro, tokens, feats)


def solution(mesh):
    return jax.shard_map(
        on_device,
        mesh=mesh,
        in_specs=(
            P(None, None, "expert", None),
            P("section", None),
            P("section", None, "expert"),
            P("section", None, "expert"),
            P("section", "expert", None),
            P(None, None, "section", "expert", None),
            P(None, None, "section", "expert", None),
        ),
        out_specs=P(None, None, "expert", "section"),
        check_vma=False,
    )
```

time: 103 us -> 116 us (1.13)
  blocking collectives: 78.9 us -> 90.3 us
  Pallas kernels: 18.4 us -> 20.1 us
    all_to_all x7 -> x9, blocking collectives: 78.9 us -> 90.3 us  [on_device(): lax.all_to_all(v, AXES, split_axis=0, concat_axis=0, tiled=True)]
    pallas_call x7 -> x9, Pallas kernels: 10.7 us -> 12.4 us  [the longest x4 7.15 us: turn(): call(functools.partial(round_kernel, **sizes), [compact(kept), flag], [VM...]
where the time goes in v1:
time: 116 us
  blocking collectives  90.3 us (78%)
  Pallas kernels  20.1 us (17%)
  starting transfers between devices  4.52 us (4%)
    all_to_all x9, blocking collectives, on_device(): lax.all_to_all(v, AXES, split_axis=0, concat_axis=0, tiled=True)  90.3 us
    pallas_call x4, Pallas kernels, turn(): call(functools.partial(round_kernel, **sizes), [compact(kept), flag], [VM...  7.15 us
    ppermute x3, starting transfers between devices, on_device(): lax.ppermute(rows[k], 'expert', [(y, (y + k) % spread) for y in range(spr...  4.52 us
    pallas_call x4, Pallas kernels, turn(): call(functools.partial(update_kernel, slots=slots, **sizes), [state, cols...  3.77 us
    pallas_call x1, Pallas kernels, on_device(): call(functools.partial(load_kernel, feats=feats), [state, resident(wg), r...  3.25 us
    pallas_call x1, Pallas kernels, on_device(): call(functools.partial(first_kernel, sections=sections, feats=feats), [me...  2.87 us
  transfers between devices with their start and end apart: 3, of which 0 were waited for; matrix products, arithmetic and copies ran while one was open for 0% of the time, Pallas kernels for 3%

profile of v1, /device:TPU:0, one launch (start us, length us, event | category | flops | bytes accessed | tf_op | source)
XLA Modules:
  0.0 115.7 jit_solution(15321239450247172899)
XLA Ops:
  0.0 1.6 %route.1 = (bf16[8,3712]{1,0:T(8,128)(2,1)S(1)}, bf16[8,3712]{1,0:T(8,128)(2,1)S(1)}, bf16[8,3712]{1,0:T(8,128)(2,1)S(1)}, bf16[8,3712]{1,0:T(8,128)(2,1)S(1)}) custom-call(s32[1]{0:T(128)} %bitcast.5.me_ref, s32[4,8,32]{2,1,0:T(8,128)} %bitcast.25, f32[4,8,32]{2,1,0:T(8,128)} %bitcast.26, bf16[128,3584]{1,0:T(8,128)(2,1)} %bitcast.20), custom_call_target="tpu_custom_call" | custom-call | tf_op jit(solution)/shard_map/route/pallas_call | solution.py:321
  1.6 0.5 collective-permute-start
  2.2 2.6 %collective-permute-start.1 = (bf16[8,3712]{1,0:T(8,128)(2,1)S(1)}, bf16[8,3712]{1,0:T(8,128)(2,1)S(1)}, u32[]{:S(2)}, u32[]{:S(2)}) collective-permute-start(bf16[8,3712]{1,0:T(8,128)(2,1)S(1)} %get-tuple-element.86), channel_id=1, source_target_pairs={{0,2},{1,3},{2,0},{3,1},{4,6},{5,7},{6,4},{7,5},{8,10},{9,11},{10,... | collective-permute-start | bytes 178184 | tf_op jit(solution)/shard_map/ppermute | solution.py:336
  4.7 1.4 %collective-permute-start.2 = (bf16[8,3712]{1,0:T(8,128)(2,1)S(1)}, bf16[8,3712]{1,0:T(8,128)(2,1)S(1)}, u32[]{:S(2)}, u32[]{:S(2)}) collective-permute-start(bf16[8,3712]{1,0:T(8,128)(2,1)S(1)} %get-tuple-element.87), channel_id=1, source_target_pairs={{0,3},{1,0},{2,1},{3,2},{4,7},{5,4},{6,5},{7,6},{8,11},{9,8},{10,9... | collective-permute-start | bytes 178184 | tf_op jit(solution)/shard_map/ppermute | solution.py:336
  6.1 0.0 copy-start.1
  6.1 3.3 %load.1 = (bf16[128,512]{1,0:T(8,128)(2,1)S(1)}, bf16[3584,512]{1,0:T(8,128)(2,1)S(1)}, bf16[3584,512]{1,0:T(8,128)(2,1)S(1)}) custom-call(s32[1]{0:T(128)} %bitcast.1.section_ref, bf16[128,3584]{1,0:T(8,128)(2,1)} %bitcast.21, bf16[3584,512]{1,0:T(8,128)(2,1)} %bitcast.22, bf16[3584,512]{1,0:T(8,128)(2,1)} %bitcast.23), custom_call_target="tpu_custom_call" | custom-call | tf_op jit(solution)/shard_map/load/pallas_call | solution.py:341
  9.4 0.0 collective-permute-done.refs_1_
  9.4 0.0 collective-permute-done.1.refs_2_
  9.4 0.0 collective-permute-done.2.refs_3_
  9.4 0.0 copy-done.1
  9.4 2.9 %first.1 = (bf16[32,8,512]{2,1,0:T(8,128)(2,1)S(1)}, bf16[512,3584]{1,0:T(8,128)(2,1)S(1)}) custom-call(s32[1]{0:T(128)} %bitcast.5.me_ref, f32[1,3584]{1,0:T(1,128)S(1)} %copy-done.1, bf16[3584,512]{1,0:T(8,128)(2,1)S(1)} %get-tuple-element.137.wg_ref, bf16[3584,512]{1,0:T(8,128)(2,1)S(1)} %get-tuple-element.138.wu_ref, bf16[512,3584]{1,0:T(8,128)(2,1)} %bitcast.24, ...), custom_call_target="tpu_custom_call" | custom-call | tf_op jit(solution)/shard_map/first/pallas_call | solution.py:353
  12.3 15.3 %all_to_all.25.in_ref = bf16[32,8,512]{2,1,0:T(8,128)(2,1)S(1)} all-to-all(bf16[32,8,512]{2,1,0:T(8,128)(2,1)S(1)} %get-tuple-element.92), channel_id=1, replica_groups=mesh['section'=8,'expert'=4] {'section','expert'}, dimensions={0} | all-to-all | bytes 524288 | tf_op jit(solution)/shard_map/all_to_all | solution.py:352
  27.6 1.5 %table.1 = (bf16[128,512]{1,0:T(8,128)(2,1)S(1)}, f32[128,128]{1,0:T(8,128)S(1)}, bf16[32,16,128]{2,1,0:T(8,128)(2,1)S(1)}, f32[128,128]{1,0:T(8,128)S(1)}) custom-call(bf16[128,512]{1,0:T(8,128)(2,1)S(1)} %get-tuple-element.91.x_ref, bf16[32,8,512]{2,1,0:T(8,128)(2,1)S(1)} %all_to_all.25.in_ref), custom_call_target="tpu_custom_call" | custom-call | tf_op jit(solution)/shard_map/table/pallas_call | solution.py:368
  29.1 10.4 %all_to_all.26.in_ref = bf16[32,16,128]{2,1,0:T(8,128)(2,1)S(1)} all-to-all(bf16[32,16,128]{2,1,0:T(8,128)(2,1)S(1)} %get-tuple-element.93), channel_id=1, replica_groups=mesh['section'=8,'expert'=4] {'section','expert'}, dimensions={0} | all-to-all | bytes 262144 | tf_op jit(solution)/shard_map/all_to_all | solution.py:352
  39.5 1.8 %round.3 = (bf16[32,16,128]{2,1,0:T(8,128)(2,1)S(1)}, s32[1]{0:T(128)S(4)}) custom-call(f32[1,3584]{1,0:T(1,128)S(1)} %copy-done.1, bf16[3584,512]{1,0:T(8,128)(2,1)S(1)} %get-tuple-element.137.wg_ref, bf16[3584,512]{1,0:T(8,128)(2,1)S(1)} %get-tuple-element.138.wu_ref, bf16[512,3584]{1,0:T(8,128)(2,1)S(1)} %get-tuple-element.139.wd_ref, ...), custom_call_target="tpu_custom_call" | custom-call | tf_op jit(solution)/shard_map/round/pallas_call | solution.py:378
  41.3 10.0 %all_to_all.27.in_ref = bf16[32,16,128]{2,1,0:T(8,128)(2,1)S(1)} all-to-all(bf16[32,16,128]{2,1,0:T(8,128)(2,1)S(1)} %get-tuple-element.97), channel_id=1, replica_groups=mesh['section'=8,'expert'=4] {'section','expert'}, dimensions={0} | all-to-all | bytes 262144 | tf_op jit(solution)/shard_map/all_to_all | solution.py:352
  51.2 1.0 update.3
  52.2 62.9 %while.15 = (s32[1]{0:T(128)S(4)}, bf16[128,512]{1,0:T(8,128)(2,1)S(1)}, f32[128,128]{1,0:T(8,128)S(1)}, bf16[32,8,128]{2,1,0:T(8,128)(2,1)S(1)}, f32[64,128]{1,...) while((s32[1]{0:T(128)S(4)}, ...), condition=%region_1.0_spmd, body=%region_0.0_spmd | while | flops 1 | bytes 262225 | solution.py:399
  52.2 9.2 %all_to_all.23.in_ref = bf16[32,8,128]{2,1,0:T(8,128)(2,1)S(1)} all-to-all(bf16[32,8,128]{2,1,0:T(8,128)(2,1)S(1)} %get-tuple-element.49), channel_id=1, replica_groups=mesh['section'=8,'expert'=4] {'section','expert'}, dimensions={0} | all-to-all | bytes 131072 | tf_op jit(solution)/shard_map/while/body/all_to_all | solution.py:352
  61.4 1.8 %round.2 = (bf16[32,8,128]{2,1,0:T(8,128)(2,1)S(1)}, s32[1]{0:T(128)S(4)}) custom-call(f32[1,3584]{1,0:T(1,128)S(1)} %get-tuple-element.154.gain_ref, bf16[3584,512]{1,0:T(8,128)(2,1)S(1)} %get-tuple-element.155.wg_ref, bf16[3584,512]{1,0:T(8,128)(2,1)S(1)} %get-tuple-element.156.wu_ref, bf16[512,3584]{1,0:T(8,128)(2,1)S(1)} %get-tuple-element.157.wd_ref, ...), custom_call_target="tpu_custom_call" | custom-call | tf_op jit(solution)/shard_map/while/body/round/pallas_call | solution.py:378
  63.2 9.1 %all_to_all.24.in_ref = bf16[32,8,128]{2,1,0:T(8,128)(2,1)S(1)} all-to-all(bf16[32,8,128]{2,1,0:T(8,128)(2,1)S(1)} %get-tuple-element.53), channel_id=1, replica_groups=mesh['section'=8,'expert'=4] {'section','expert'}, dimensions={0} | all-to-all | bytes 131072 | tf_op jit(solution)/shard_map/while/body/all_to_all | solution.py:352
  72.3 0.9 update.2
  73.2 9.1 %all_to_all.23.in_ref = bf16[32,8,128]{2,1,0:T(8,128)(2,1)S(1)} all-to-all(bf16[32,8,128]{2,1,0:T(8,128)(2,1)S(1)} %get-tuple-element.49), channel_id=1, replica_groups=mesh['section'=8,'expert'=4] {'section','expert'}, dimensions={0} | all-to-all | bytes 131072 | tf_op jit(solution)/shard_map/while/body/all_to_all | solution.py:352
  82.3 1.8 %round.2 = (bf16[32,8,128]{2,1,0:T(8,128)(2,1)S(1)}, s32[1]{0:T(128)S(4)}) custom-call(f32[1,3584]{1,0:T(1,128)S(1)} %get-tuple-element.154.gain_ref, bf16[3584,512]{1,0:T(8,128)(2,1)S(1)} %get-tuple-element.155.wg_ref, bf16[3584,512]{1,0:T(8,128)(2,1)S(1)} %get-tuple-element.156.wu_ref, bf16[512,3584]{1,0:T(8,128)(2,1)S(1)} %get-tuple-element.157.wd_ref, ...), custom_call_target="tpu_custom_call" | custom-call | tf_op jit(solution)/shard_map/while/body/round/pallas_call | solution.py:378
  84.1 9.1 %all_to_all.24.in_ref = bf16[32,8,128]{2,1,0:T(8,128)(2,1)S(1)} all-to-all(bf16[32,8,128]{2,1,0:T(8,128)(2,1)S(1)} %get-tuple-element.53), channel_id=1, replica_groups=mesh['section'=8,'expert'=4] {'section','expert'}, dimensions={0} | all-to-all | bytes 131072 | tf_op jit(solution)/shard_map/while/body/all_to_all | solution.py:352
  93.2 0.9 update.2
  94.2 9.1 %all_to_all.23.in_ref = bf16[32,8,128]{2,1,0:T(8,128)(2,1)S(1)} all-to-all(bf16[32,8,128]{2,1,0:T(8,128)(2,1)S(1)} %get-tuple-element.49), channel_id=1, replica_groups=mesh['section'=8,'expert'=4] {'section','expert'}, dimensions={0} | all-to-all | bytes 131072 | tf_op jit(solution)/shard_map/while/body/all_to_all | solution.py:352
  103.3 1.8 %round.2 = (bf16[32,8,128]{2,1,0:T(8,128)(2,1)S(1)}, s32[1]{0:T(128)S(4)}) custom-call(f32[1,3584]{1,0:T(1,128)S(1)} %get-tuple-element.154.gain_ref, bf16[3584,512]{1,0:T(8,128)(2,1)S(1)} %get-tuple-element.155.wg_ref, bf16[3584,512]{1,0:T(8,128)(2,1)S(1)} %get-tuple-element.156.wu_ref, bf16[512,3584]{1,0:T(8,128)(2,1)S(1)} %get-tuple-element.157.wd_ref, ...), custom_call_target="tpu_custom_call" | custom-call | tf_op jit(solution)/shard_map/while/body/round/pallas_call | solution.py:378
  105.0 9.1 %all_to_all.24.in_ref = bf16[32,8,128]{2,1,0:T(8,128)(2,1)S(1)} all-to-all(bf16[32,8,128]{2,1,0:T(8,128)(2,1)S(1)} %get-tuple-element.53), channel_id=1, replica_groups=mesh['section'=8,'expert'=4] {'section','expert'}, dimensions={0} | all-to-all | bytes 131072 | tf_op jit(solution)/shard_map/while/body/all_to_all | solution.py:352
  114.1 0.9 update.2
  115.1 0.0 copy-start
  115.1 0.6 copy-done
Async XLA Ops:
  1.6 7.8 %collective-permute-start = (bf16[8,3712]{1,0:T(8,128)(2,1)S(1)}, bf16[8,3712]{1,0:T(8,128)(2,1)S(1)}, u32[]{:S(2)}, u32[]{:S(2)}) collective-permute-start(bf16[8,3712]{1,0:T(8,128)(2,1)S(1)} %get-tuple-element.85), channel_id=1, source_target_pairs={{0,1},{1,2},{2,3},{3,0},{4,5},{5,6},{6,7},{7,4},{8,9},{9,10},{10,1... | collective-permute-start | bytes 178184 | tf_op jit(solution)/shard_map/ppermute | solution.py:336
  2.2 7.2 %collective-permute-start.1 = (bf16[8,3712]{1,0:T(8,128)(2,1)S(1)}, bf16[8,3712]{1,0:T(8,128)(2,1)S(1)}, u32[]{:S(2)}, u32[]{:S(2)}) collective-permute-start(bf16[8,3712]{1,0:T(8,128)(2,1)S(1)} %get-tuple-element.86), channel_id=1, source_target_pairs={{0,2},{1,3},{2,0},{3,1},{4,6},{5,7},{6,4},{7,5},{8,10},{9,11},{10,... | collective-permute-start | bytes 178184 | tf_op jit(solution)/shard_map/ppermute | solution.py:336
  4.7 4.7 %collective-permute-start.2 = (bf16[8,3712]{1,0:T(8,128)(2,1)S(1)}, bf16[8,3712]{1,0:T(8,128)(2,1)S(1)}, u32[]{:S(2)}, u32[]{:S(2)}) collective-permute-start(bf16[8,3712]{1,0:T(8,128)(2,1)S(1)} %get-tuple-element.87), channel_id=1, source_target_pairs={{0,3},{1,0},{2,1},{3,2},{4,7},{5,4},{6,5},{7,6},{8,11},{9,8},{10,9... | collective-permute-start | bytes 178184 | tf_op jit(solution)/shard_map/ppermute | solution.py:336
  6.1 3.3 %copy-start.1 = (f32[1,3584]{1,0:T(1,128)S(1)}, f32[1,3584]{1,0:T(1,128)}, u32[]{:S(2)}) copy-start(f32[1,3584]{1,0:T(1,128)} %gain_ref.3) | copy-start | bytes 43012
  115.1 0.7 copy-start
